TPU v7x, 32 devices: a whole 2x2x4 slice. The times are simulated.
32 devices in a mesh: query: 4 (over x, core), db: 8 (over z, y).
Axes of the slice: x: 2, y: 2, z: 4, core: 2. Of those that a mesh axis runs over, the one named last changes fastest.
Arguments:
- logits: bfloat16 [20, 1048576], P(None, ('query', 'db')), may hold values from -40 to 340
- entry_ids: int32 [1048576], P(('query', 'db')), may hold values from 0 to 8191, as said below
- query_counts: bfloat16 [4096, 2400], P(('query', 'db')), may hold values from 0.0099 to 1
- idf_weights: float32 [2400], replicated, may hold values from 0.05 to 5
Outputs:
- block_max: float32 [16, 4096], P('db', 'query')
Inputs may be any that keep to these rules, and one draw needn't show every extreme that they name: `entry_ids`: never falling; every entry 0 to 8191 has 32 or more residues, and some entry exactly 32. Shard s = q * 8 + d holds residues s * 32768 to (s + 1) * 32768 - 1, and no entry crosses a shard's edge. The shards of query index q together hold entries q * 2048 to (q + 1) * 2048 - 1; a shard holds at most 448 entries, and in every query index some shard holds exactly 448.
All inputs are finite; a program needn't handle non-finite values.
Results may differ from a plain program's by a relative error of at most 0.00074.
Values may be sent and summed in bfloat16 or wider, within the bound.
A program may use at most 64 MiB of HBM per device.

v0:
```python
import math

import jax
import jax.numpy as jnp
from jax import lax
from jax.sharding import PartitionSpec as P

OFFSETS = 6
FEAT = 2400
E_DEV = 1024
LMIN = 32
BR = 256
BLOCK = 512


EPSILON = 1e-06


def normalized(counts, idf_weights):
    scaled = counts.astype(jnp.float32) * idf_weights
    return (scaled / jnp.sqrt(jnp.sum(scaled * scaled, axis=-1, keepdims=True) + EPSILON)).astype(
        jnp.bfloat16
    )


def encode(logits, entry_ids, table_rows):
    states, residues = logits.shape
    window = BR // LMIN + 1
    state_probs = jax.nn.softmax(logits.astype(jnp.float32), axis=0).astype(jnp.bfloat16)
    local_ids = entry_ids - entry_ids[0]
    padded = jnp.pad(state_probs, ((0, 0), (0, OFFSETS)))
    padded_ids = jnp.pad(local_ids, (0, OFFSETS), constant_values=-1)
    blocks = residues // BR
    group_size = math.gcd(blocks, 16)
    span = group_size * BR
    columns = jnp.arange(window, dtype=jnp.int32)

    def add_group(counts_table, group_index):
        first_res = group_index * span
        prob_slab = lax.dynamic_slice_in_dim(padded, first_res, span + OFFSETS, 1)
        id_slab = lax.dynamic_slice_in_dim(padded_ids, first_res, span + OFFSETS, 0)
        own_ids = id_slab[:span]
        partner_rows = []
        for offset in range(OFFSETS):
            same_entry = id_slab[offset + 1 : offset + 1 + span] == own_ids
            partner_rows.append(
                jnp.where(
                    same_entry[None, :],
                    prob_slab[:, offset + 1 : offset + 1 + span],
                    jnp.zeros((), jnp.bfloat16),
                )
            )
        partner_part = jnp.stack(partner_rows, axis=0).reshape(OFFSETS * states, group_size, BR)
        prob_part = prob_slab[:, :span].reshape(states, group_size, BR)
        id_blocks = own_ids.reshape(group_size, BR)
        start_part = id_blocks[:, 0]
        rel_part = id_blocks - start_part[:, None]
        onehot = rel_part[:, None, :] == columns[None, :, None]
        spread = jnp.where(
            onehot[:, :, None, :],
            prob_part.transpose(1, 0, 2)[:, None, :, :],
            jnp.zeros((), jnp.bfloat16),
        )
        pair_sums = jnp.einsum(
            "nwsr,cnr->nwsc", spread, partner_part, preferred_element_type=jnp.float32
        )
        targets = (start_part[:, None] + columns[None, :]).reshape(-1)
        counts_table = counts_table.at[targets].add(pair_sums.reshape(-1, FEAT))
        return (counts_table, None)

    empty_table = jnp.zeros((table_rows + window, FEAT), jnp.float32)
    counts_table, _ = lax.scan(
        add_group, empty_table, jnp.arange(blocks // group_size, dtype=jnp.int32)
    )
    return (counts_table[:table_rows], entry_ids[0], local_ids[-1] + 1)


def on_device(logits, entry_ids, query_counts, idf_weights):
    db_count = lax.axis_size("db")
    query_count = lax.axis_size("query")
    query_index = lax.axis_index("query")
    share_rows = E_DEV // query_count
    most_rows = share_rows + 3 * share_rows // 4
    slot_count = -(-most_rows // db_count)
    blocks_here = E_DEV // BLOCK
    query_rows = normalized(query_counts, idf_weights)
    counts_table, first_entry, entry_total = encode(logits, entry_ids, most_rows)
    db_rows = normalized(counts_table, idf_weights)
    owner_first = jnp.mod(jnp.arange(db_count, dtype=jnp.int32) - first_entry, db_count)
    picked = owner_first[:, None] + db_count * jnp.arange(slot_count, dtype=jnp.int32)[None, :]
    usable = picked < entry_total
    chosen = jnp.take(db_rows, jnp.minimum(picked, most_rows - 1), axis=0)
    outgoing = jnp.where(usable[:, :, None], chosen, jnp.zeros((), jnp.bfloat16))
    targets = jnp.where(
        usable, (first_entry + picked - query_index * share_rows * db_count) // db_count, -1
    )
    arrived, places = (
        lax.all_to_all(outgoing, "db", split_axis=0, concat_axis=0, tiled=True),
        lax.all_to_all(targets, "db", split_axis=0, concat_axis=0, tiled=True),
    )
    places = places.reshape(-1)
    owned_rows = (
        jnp.zeros((share_rows + 1, FEAT), jnp.bfloat16)
        .at[jnp.where(places >= 0, places, share_rows)]
        .set(arrived.reshape(-1, FEAT))[:share_rows]
    )
    replicas = lax.all_gather(owned_rows, "query", axis=0, tiled=True)
    segment = lax.all_gather(query_rows, "db", axis=0, tiled=True)
    scores = lax.dot_general(
        replicas, segment, (((1,), (1,)), ((), ())), preferred_element_type=jnp.float32
    )
    return jnp.max(scores.reshape(blocks_here, BLOCK, segment.shape[0]), axis=1)


def solution(mesh):
    placed = (P(None, ("query", "db")), P(("query", "db")), P(("query", "db"), None), P())
    return jax.shard_map(
        on_device, mesh=mesh, in_specs=placed, out_specs=P("db", "query"), check_vma=False
    )
```

profile of v0, /device:TPU:0, one launch (start us, length us, event | category | flops | bytes accessed | tf_op | source)
XLA Modules:
  0.0 286.6 jit_solution(2304918433274222863)
XLA Ops:
  6.5 1.4 slice.58
  7.9 1.6 broadcast_subtract_fusion.1
  12.9 7.3 %all-to-all-start = ((s32[8,1,56]{2,1,0:T(1,128)}), s32[8,1,56]{2,1,0:T(1,128)S(1)}, u32[]{:S(2)}, u32[]{:S(2)}) async-start(s32[8,1,56]{2,1,0:T(1,128)} %compare_select_fusion.1), calls=%async_computation | async-start | bytes 8192 | tf_op jit(solution)/shard_map/all_to_all | solution.py:99
  20.2 1.5 multiply_reduce_fusion.1
  21.7 2.3 divide_convert_fusion.2
  26.1 2.4 broadcast_in_dim.122
  28.5 130.6 %while.12 = (s32[]{:T(128)}, f32[457,2400]{1,0:T(8,128)}, s32[8]{0:T(128)S(1)}, s32[32774]{0:T(1024)S(1)}, bf16[20,32774]{1,0:T(8,128)(2,1)S(1)}, /*index=5*/s32...) while((s32[]{:T(128)}, f32[457,2400]{1,0:T(8,128)}, ...), condition=%wide.region_4.5_spmd.clone.clone, body=%wide.region_2.4_spmd.clone.clone.sunk | while | flops 178587728 | bytes 15466447 | solution.py:72
  31.0 1.4 reshape.408
  32.7 3.3 %fusion.48 = f32[16,9,20,120]{3,2,1,0:T(8,128)} fusion(pred[16,9,256]{2,1,0:T(8,128)(4,1)S(1)} %iota_compare_fusion.2, bf16[120,16,256,1]{2,1,0,3:T(8,128)(2,1)} %bitcast.67, bf16[16,20,256]{2,1,0:T(8,128)(2,1)S(1)} %copy.22), kind=kOutput, calls=%fused_computation.4.clone.1 | convolution fusion | flops 177684480 | bytes 2566144 | tf_op jit(solution)/shard_map/while/body/eval_jaxpr/nwsr,cnr->nwsc/dot_general | solution.py:64
  36.0 1.8 reshape.409
  37.9 7.0 %scatter_fusion = f32[457,2400]{1,0:T(8,128)} fusion(f32[457,2400]{1,0:T(8,128)} %get-tuple-element.149, s32[144]{0:T(256)S(1)} %bitcast.72, f32[144,2400]{1,0:T(8,128)S(1)} %reshape.409), kind=kCustom, calls=%fused_computation.1.clone.clone.1 | custom fusion | flops 345600 | bytes 4147776 | tf_op jit(solution)/shard_map/while/body/eval_jaxpr/scatter-add | solution.py:68
  47.4 1.4 reshape.408
  49.1 3.2 %fusion.48 = f32[16,9,20,120]{3,2,1,0:T(8,128)} fusion(pred[16,9,256]{2,1,0:T(8,128)(4,1)S(1)} %iota_compare_fusion.2, bf16[120,16,256,1]{2,1,0,3:T(8,128)(2,1)} %bitcast.67, bf16[16,20,256]{2,1,0:T(8,128)(2,1)S(1)} %copy.22), kind=kOutput, calls=%fused_computation.4.clone.1 | convolution fusion | flops 177684480 | bytes 2566144 | tf_op jit(solution)/shard_map/while/body/eval_jaxpr/nwsr,cnr->nwsc/dot_general | solution.py:64
  52.3 1.8 reshape.409
  54.2 7.0 %scatter_fusion = f32[457,2400]{1,0:T(8,128)} fusion(f32[457,2400]{1,0:T(8,128)} %get-tuple-element.149, s32[144]{0:T(256)S(1)} %bitcast.72, f32[144,2400]{1,0:T(8,128)S(1)} %reshape.409), kind=kCustom, calls=%fused_computation.1.clone.clone.1 | custom fusion | flops 345600 | bytes 4147776 | tf_op jit(solution)/shard_map/while/body/eval_jaxpr/scatter-add | solution.py:68
  63.8 1.4 reshape.408
  65.4 3.3 %fusion.48 = f32[16,9,20,120]{3,2,1,0:T(8,128)} fusion(pred[16,9,256]{2,1,0:T(8,128)(4,1)S(1)} %iota_compare_fusion.2, bf16[120,16,256,1]{2,1,0,3:T(8,128)(2,1)} %bitcast.67, bf16[16,20,256]{2,1,0:T(8,128)(2,1)S(1)} %copy.22), kind=kOutput, calls=%fused_computation.4.clone.1 | convolution fusion | flops 177684480 | bytes 2566144 | tf_op jit(solution)/shard_map/while/body/eval_jaxpr/nwsr,cnr->nwsc/dot_general | solution.py:64
  68.7 1.8 reshape.409
  70.6 7.0 %scatter_fusion = f32[457,2400]{1,0:T(8,128)} fusion(f32[457,2400]{1,0:T(8,128)} %get-tuple-element.149, s32[144]{0:T(256)S(1)} %bitcast.72, f32[144,2400]{1,0:T(8,128)S(1)} %reshape.409), kind=kCustom, calls=%fused_computation.1.clone.clone.1 | custom fusion | flops 345600 | bytes 4147776 | tf_op jit(solution)/shard_map/while/body/eval_jaxpr/scatter-add | solution.py:68
  80.1 1.4 reshape.408
  81.8 3.2 %fusion.48 = f32[16,9,20,120]{3,2,1,0:T(8,128)} fusion(pred[16,9,256]{2,1,0:T(8,128)(4,1)S(1)} %iota_compare_fusion.2, bf16[120,16,256,1]{2,1,0,3:T(8,128)(2,1)} %bitcast.67, bf16[16,20,256]{2,1,0:T(8,128)(2,1)S(1)} %copy.22), kind=kOutput, calls=%fused_computation.4.clone.1 | convolution fusion | flops 177684480 | bytes 2566144 | tf_op jit(solution)/shard_map/while/body/eval_jaxpr/nwsr,cnr->nwsc/dot_general | solution.py:64
  85.0 1.8 reshape.409
  86.9 7.0 %scatter_fusion = f32[457,2400]{1,0:T(8,128)} fusion(f32[457,2400]{1,0:T(8,128)} %get-tuple-element.149, s32[144]{0:T(256)S(1)} %bitcast.72, f32[144,2400]{1,0:T(8,128)S(1)} %reshape.409), kind=kCustom, calls=%fused_computation.1.clone.clone.1 | custom fusion | flops 345600 | bytes 4147776 | tf_op jit(solution)/shard_map/while/body/eval_jaxpr/scatter-add | solution.py:68
  96.4 1.4 reshape.408
  98.1 3.2 %fusion.48 = f32[16,9,20,120]{3,2,1,0:T(8,128)} fusion(pred[16,9,256]{2,1,0:T(8,128)(4,1)S(1)} %iota_compare_fusion.2, bf16[120,16,256,1]{2,1,0,3:T(8,128)(2,1)} %bitcast.67, bf16[16,20,256]{2,1,0:T(8,128)(2,1)S(1)} %copy.22), kind=kOutput, calls=%fused_computation.4.clone.1 | convolution fusion | flops 177684480 | bytes 2566144 | tf_op jit(solution)/shard_map/while/body/eval_jaxpr/nwsr,cnr->nwsc/dot_general | solution.py:64
  101.3 1.8 reshape.409
  103.2 7.0 %scatter_fusion = f32[457,2400]{1,0:T(8,128)} fusion(f32[457,2400]{1,0:T(8,128)} %get-tuple-element.149, s32[144]{0:T(256)S(1)} %bitcast.72, f32[144,2400]{1,0:T(8,128)S(1)} %reshape.409), kind=kCustom, calls=%fused_computation.1.clone.clone.1 | custom fusion | flops 345600 | bytes 4147776 | tf_op jit(solution)/shard_map/while/body/eval_jaxpr/scatter-add | solution.py:68
  112.7 1.4 reshape.408
  114.4 3.2 %fusion.48 = f32[16,9,20,120]{3,2,1,0:T(8,128)} fusion(pred[16,9,256]{2,1,0:T(8,128)(4,1)S(1)} %iota_compare_fusion.2, bf16[120,16,256,1]{2,1,0,3:T(8,128)(2,1)} %bitcast.67, bf16[16,20,256]{2,1,0:T(8,128)(2,1)S(1)} %copy.22), kind=kOutput, calls=%fused_computation.4.clone.1 | convolution fusion | flops 177684480 | bytes 2566144 | tf_op jit(solution)/shard_map/while/body/eval_jaxpr/nwsr,cnr->nwsc/dot_general | solution.py:64
  117.6 1.8 reshape.409
  119.5 7.0 %scatter_fusion = f32[457,2400]{1,0:T(8,128)} fusion(f32[457,2400]{1,0:T(8,128)} %get-tuple-element.149, s32[144]{0:T(256)S(1)} %bitcast.72, f32[144,2400]{1,0:T(8,128)S(1)} %reshape.409), kind=kCustom, calls=%fused_computation.1.clone.clone.1 | custom fusion | flops 345600 | bytes 4147776 | tf_op jit(solution)/shard_map/while/body/eval_jaxpr/scatter-add | solution.py:68
  129.0 1.4 reshape.408
  130.7 3.2 %fusion.48 = f32[16,9,20,120]{3,2,1,0:T(8,128)} fusion(pred[16,9,256]{2,1,0:T(8,128)(4,1)S(1)} %iota_compare_fusion.2, bf16[120,16,256,1]{2,1,0,3:T(8,128)(2,1)} %bitcast.67, bf16[16,20,256]{2,1,0:T(8,128)(2,1)S(1)} %copy.22), kind=kOutput, calls=%fused_computation.4.clone.1 | convolution fusion | flops 177684480 | bytes 2566144 | tf_op jit(solution)/shard_map/while/body/eval_jaxpr/nwsr,cnr->nwsc/dot_general | solution.py:64
  133.9 1.8 reshape.409
  135.8 7.0 %scatter_fusion = f32[457,2400]{1,0:T(8,128)} fusion(f32[457,2400]{1,0:T(8,128)} %get-tuple-element.149, s32[144]{0:T(256)S(1)} %bitcast.72, f32[144,2400]{1,0:T(8,128)S(1)} %reshape.409), kind=kCustom, calls=%fused_computation.1.clone.clone.1 | custom fusion | flops 345600 | bytes 4147776 | tf_op jit(solution)/shard_map/while/body/eval_jaxpr/scatter-add | solution.py:68
  145.3 1.4 reshape.408
  147.0 3.2 %fusion.48 = f32[16,9,20,120]{3,2,1,0:T(8,128)} fusion(pred[16,9,256]{2,1,0:T(8,128)(4,1)S(1)} %iota_compare_fusion.2, bf16[120,16,256,1]{2,1,0,3:T(8,128)(2,1)} %bitcast.67, bf16[16,20,256]{2,1,0:T(8,128)(2,1)S(1)} %copy.22), kind=kOutput, calls=%fused_computation.4.clone.1 | convolution fusion | flops 177684480 | bytes 2566144 | tf_op jit(solution)/shard_map/while/body/eval_jaxpr/nwsr,cnr->nwsc/dot_general | solution.py:64
  150.2 1.8 reshape.409
  152.1 7.0 %scatter_fusion = f32[457,2400]{1,0:T(8,128)} fusion(f32[457,2400]{1,0:T(8,128)} %get-tuple-element.149, s32[144]{0:T(256)S(1)} %bitcast.72, f32[144,2400]{1,0:T(8,128)S(1)} %reshape.409), kind=kCustom, calls=%fused_computation.1.clone.clone.1 | custom fusion | flops 345600 | bytes 4147776 | tf_op jit(solution)/shard_map/while/body/eval_jaxpr/scatter-add | solution.py:68
  159.2 2.8 multiply_reduce_fusion
  162.0 2.8 divide_convert_fusion
  164.8 3.4 %gather_fusion = bf16[448,2400]{1,0:T(8,128)(2,1)} fusion(bf16[448,2400]{1,0:T(8,128)(2,1)S(1)} %divide_convert_fusion, s32[1024]{0:T(1024)S(1)} %pad_clamp_fusion), kind=kCustom, calls=%fused_computation | custom fusion | bytes 4302592 | tf_op jit(solution)/shard_map/jit(_take)/gather | solution.py:92
  168.2 3.5 %select_select_fusion = bf16[8,56,2400]{2,1,0:T(8,128)(2,1)} fusion(bf16[8,56,2400]{2,1,0:T(8,128)(2,1)} %bitcast.70, pred[8,56]{1,0:T(8,128)(4,1)S(1)} %get-tuple-element.87, pred[8,56]{1,0:T(8,128)(4,1)S(1)} %get-tuple-element.86), kind=kLoop, calls=%fused_computation.49 | loop fusion | flops 2150400 | bytes 4301696 | tf_op jit(solution)/shard_map/jit(_where)/select_n | solution.py:93
  171.7 5.9 %all-to-all-start.1 = ((bf16[8,56,2400]{2,1,0:T(8,128)(2,1)}), bf16[8,56,2400]{2,1,0:T(8,128)(2,1)S(1)}, u32[]{:S(2)}, u32[]{:S(2)}) async-start(bf16[8,56,2400]{2,1,0:T(8,128)(2,1)} %select_select_fusion), calls=%async_computation.1 | async-start | bytes 4358144 | tf_op jit(solution)/shard_map/all_to_all | solution.py:98
  179.1 48.0 %all-to-all-done.1 = bf16[8,56,2400]{2,1,0:T(8,128)(2,1)S(1)} async-done(((bf16[8,56,2400]{2,1,0:T(8,128)(2,1)}), bf16[8,56,2400]{2,1,0:T(8,128)(2,1)S(1)}, u32[]{:S(2)}, u32[]{:S(2)}) %all-to-all-start.1) | async-done | bytes 2150432 | tf_op jit(solution)/shard_map/all_to_all | solution.py:98
  227.1 3.9 %scatter_custom_fusion.1 = bf16[257,2400]{1,0:T(8,128)(2,1)S(1)} fusion(s32[448]{0:T(512)S(1)} %bitcast.73, bf16[448,2400]{1,0:T(8,128)(2,1)S(1)} %bitcast.71, bf16[]{:T(256)} %constant.53.clone.1), kind=kCustom, calls=%fused_computation.53 | custom fusion | bytes 1233602 | tf_op jit(solution)/shard_map/scatter | solution.py:105
  232.2 38.1 %all-gather.3.cloned.1.call-done = bf16[1024,2400]{1,0:T(8,128)(2,1)} async-done(((bf16[256,2400]{1,0:T(8,128)(2,1)}), bf16[1024,2400]{1,0:T(8,128)(2,1)}) %all-gather.3.cloned.1.call-update) | async-done | bytes 4915216 | tf_op jit(solution)/shard_map/all_gather | solution.py:107
  270.3 9.5 %bitcast_reduce_fusion = f32[2,1024]{1,0:T(2,128)} fusion(bf16[1024,2400]{1,0:T(8,128)(2,1)} %all-gather.3.cloned.1.call-done, bf16[1024,2400]{0,1:T(8,128)(2,1)} %all-gather.5.cloned.1.call-done), kind=kOutput, calls=%fused_computation.45 | convolution fusion | flops 5034211328 | bytes 9838592 | tf_op jit(solution)/shard_map/dot_general | solution.py:109
  (192 shorter events, 24.9 us)
Async XLA Ops:
  6.5 17.5 %copy-start = (bf16[20,32768]{1,0:T(8,128)(2,1)S(1)}, bf16[20,32768]{1,0:T(8,128)(2,1)}, u32[]{:S(2)}) copy-start(bf16[20,32768]{1,0:T(8,128)(2,1)} %param.6) | copy-start | bytes 3932164
  12.9 158.8 %all-to-all-start = ((s32[8,1,56]{2,1,0:T(1,128)}), s32[8,1,56]{2,1,0:T(1,128)S(1)}, u32[]{:S(2)}, u32[]{:S(2)}) async-start(s32[8,1,56]{2,1,0:T(1,128)} %compare_select_fusion.1), calls=%async_computation | async-start | bytes 8192 | tf_op jit(solution)/shard_map/all_to_all | solution.py:99
  20.2 212.0 %all-gather.5.cloned.1.call-start = ((), (), s32[]{:S(2)}) async-start(), calls=%async_computation.3 | async-start | bytes 5529600 | tf_op jit(solution)/shard_map/all_gather | solution.py:108
  28.5 130.7 %copy-start.1 = (f32[2400]{0:T(1024)S(1)}, f32[2400]{0:T(1024)}, u32[]{:S(2)}) copy-start(f32[2400]{0:T(1024)} %param.9) | copy-start | bytes 28804
  171.7 55.4 %all-to-all-start.1 = ((bf16[8,56,2400]{2,1,0:T(8,128)(2,1)}), bf16[8,56,2400]{2,1,0:T(8,128)(2,1)S(1)}, u32[]{:S(2)}, u32[]{:S(2)}) async-start(bf16[8,56,2400]{2,1,0:T(8,128)(2,1)} %select_select_fusion), calls=%async_computation.1 | async-start | bytes 4358144 | tf_op jit(solution)/shard_map/all_to_all | solution.py:98
  177.6 92.7 %all-gather.3.cloned.1.call-start = ((), (), s32[]{:S(2)}) async-start(), calls=%async_computation.2 | async-start | bytes 6225920 | tf_op jit(solution)/shard_map/all_gather | solution.py:107
Sparse Core Ops, SparseCore 0:
  24.2 84.2 all-gather.4
  232.3 37.9 all-gather.2
where the time goes:
time: 288 us; the launch traced here: 287 us
  waiting for transfers between devices  86.1 us (30%)
  other arithmetic  84.6 us (29%)
  local copies, waits for them, and re-layouts  47.4 us (16%)
  matrix products  35.5 us (12%)
  between operations  14.2 us (5%)
  starting transfers between devices  13.5 us (5%)
  loops' own time  5.37 us (2%)
    scatter-add x8, other arithmetic, add_group(): counts_table = counts_table.at[targets].add(pair_sums.reshape(-1, FEAT))  56 us
    all_to_all x1, waiting for transfers between devices, on_device(): lax.all_to_all(outgoing, 'db', split_axis=0, concat_axis=0, tiled=True)  48 us
    all_gather x1, waiting for transfers between devices, on_device(): replicas = lax.all_gather(owned_rows, 'query', axis=0, tiled=True)  38.1 us
    dot_general x8, matrix products, add_group(): jnp.einsum('nwsr,cnr->nwsc', spread, partner_part, preferred_element_type...  26 us
    reshape x8, local copies, waits for them, and re-layouts, add_group(): counts_table = counts_table.at[targets].add(pair_sums.reshape(-1, FEAT))  14.6 us
    reshape x8, local copies, waits for them, and re-layouts, add_group(): jnp.stack(partner_rows, axis=0).reshape(OFFSETS * states, group_size, BR)  11.3 us
    dot_general x1, matrix products, on_device(): lax.dot_general(replicas, segment, (((1,), (1,)), ((), ())), preferred_el...  9.53 us
    all_to_all x1, starting transfers between devices, on_device(): lax.all_to_all(targets, 'db', split_axis=0, concat_axis=0, tiled=True)  7.31 us
  transfers between devices with their start and end apart: 4, of which 2 were waited for; matrix products, arithmetic and copies ran while one was open for 53% of the time, Pallas kernels for 0%

commit v1 on v0

v1 whole, which is shorter than its diff:
```python
import functools

import jax
import jax.numpy as jnp
from jax import lax
from jax.experimental import pallas as pl
from jax.experimental.pallas import tpu as pltpu
from jax.sharding import PartitionSpec as P

STATES = 20
OFFSETS = 6
COLS = STATES * OFFSETS
LANES = 128
BR = 256
WINDOW = 16
E_DEV = 1024
HALVES = 2
CORES = 2
EPSILON = 1e-06
HALO = 128


def align_up(value, unit):
    return -(-value // unit) * unit


def encode_kernel(
    residues, rows, chunk, starts_ref, logits_ref, ids_ref, idf_ref, out_ref, probs, partner, table
):
    table[...] = jnp.zeros_like(table)
    partner[COLS:, :] = jnp.zeros((LANES - COLS, chunk), jnp.float32)
    probs[:, residues:] = jnp.zeros((STATES, HALO), jnp.float32)

    def soften(step, carry):
        cols = pl.ds(pl.multiple_of(step * chunk, chunk), chunk)
        values = logits_ref[:, cols].astype(jnp.float32)
        values = jnp.exp(values - jnp.max(values, axis=0, keepdims=True))
        values = values / jnp.sum(values, axis=0, keepdims=True)
        probs[:, cols] = values.astype(jnp.bfloat16).astype(jnp.float32)
        return carry

    lax.fori_loop(0, residues // chunk, soften, 0)
    slots = lax.broadcasted_iota(jnp.int32, (WINDOW, BR), 0)

    def add_chunk(step, carry):
        first = pl.multiple_of(step * chunk, chunk)
        wide = pl.ds(first, chunk + HALO)
        prob_slab = probs[:, wide]
        id_slab = ids_ref[:, wide]
        own_ids = id_slab[:, :chunk]
        for offset in range(OFFSETS):
            shift = chunk + HALO - offset - 1
            moved = pltpu.roll(prob_slab, shift, 1)[:, :chunk]
            moved_ids = pltpu.roll(id_slab, shift, 1)[:, :chunk]
            partner[offset * STATES : (offset + 1) * STATES, :] = jnp.where(
                moved_ids == own_ids, moved, 0.0
            )
        for block in range(chunk // BR):
            here = slice(block * BR, (block + 1) * BR)
            base = pl.multiple_of(starts_ref[step * (chunk // BR) + block], 8)
            onehot = (own_ids[:, here] - base) == slots
            spread = jnp.concatenate(
                [
                    jnp.where(onehot, prob_slab[a : a + 1, here], 0.0).astype(jnp.bfloat16)
                    for a in range(STATES)
                ],
                axis=0,
            )
            sums = lax.dot_general(
                spread,
                partner[:, here].astype(jnp.bfloat16),
                (((1,), (1,)), ((), ())),
                preferred_element_type=jnp.float32,
            )
            for a in range(STATES):
                table[a, pl.ds(base, WINDOW), :] += sums[a * WINDOW : (a + 1) * WINDOW]
        return carry

    lax.fori_loop(0, residues // chunk, add_chunk, 0)

    def finish(step, carry):
        part = pl.ds(pl.multiple_of(step * 16, 16), 16)
        total = jnp.zeros((16, LANES), jnp.float32)
        for a in range(STATES):
            scaled = table[a, part, :] * idf_ref[a : a + 1, :]
            total += scaled * scaled
        norm = jnp.sqrt(jnp.sum(total, axis=1, keepdims=True) + EPSILON)
        for a in range(STATES):
            scaled = table[a, part, :] * idf_ref[a : a + 1, :]
            out_ref[part, a * LANES : (a + 1) * LANES] = (scaled / norm).astype(jnp.bfloat16)
        return carry

    lax.fori_loop(0, rows // 16, finish, 0)


def encode(logits, entry_ids, idf_pad, rows, db_count):
    residues = logits.shape[1]
    chunk = min(2048, residues)
    first = entry_ids[0]
    local_ids = entry_ids - (first - lax.rem(first, db_count))
    starts = jnp.clip(local_ids[::BR] // 8 * 8, 0, rows - WINDOW)
    padded_ids = jnp.pad(local_ids, (0, HALO), constant_values=-1)[None, :]
    vmem = pl.BlockSpec(memory_space=pltpu.VMEM)
    return pl.pallas_call(
        functools.partial(encode_kernel, residues, rows, chunk),
        out_shape=jax.ShapeDtypeStruct((rows, STATES * LANES), jnp.bfloat16),
        in_specs=[pl.BlockSpec(memory_space=pltpu.SMEM), vmem, vmem, vmem],
        out_specs=vmem,
        scratch_shapes=[
            pltpu.VMEM((STATES, residues + HALO), jnp.float32),
            pltpu.VMEM((LANES, chunk), jnp.float32),
            pltpu.VMEM((STATES, rows, LANES), jnp.float32),
        ],
        cost_estimate=pl.CostEstimate(
            flops=2 * residues * STATES * WINDOW * LANES,
            bytes_accessed=residues * 44 + rows * STATES * LANES * 2,
            transcendentals=residues * STATES,
        ),
        compiler_params=pltpu.CompilerParams(vmem_limit_bytes=32 * 1024 * 1024),
        name="encode",
    )(starts, logits, padded_ids, idf_pad)


def pad_features(values):
    lead = values.shape[:-1]
    split = values.reshape(lead + (STATES, COLS))
    return jnp.pad(split, ((0, 0),) * (len(lead) + 1) + ((0, LANES - COLS),))


def on_device(logits, entry_ids, query_counts, idf_weights):
    db_count = lax.axis_size("db")
    query_count = lax.axis_size("query")
    chips = query_count // CORES
    chip = lax.axis_index("query") // CORES
    share_rows = E_DEV // query_count
    most_rows = share_rows + 3 * share_rows // 4
    rows = align_up(most_rows + db_count, max(16, db_count))

    scaled = query_counts.astype(jnp.float32) * idf_weights
    query_rows = (
        scaled / jnp.sqrt(jnp.sum(scaled * scaled, axis=-1, keepdims=True) + EPSILON)
    ).astype(jnp.bfloat16)
    query_rows = pad_features(query_rows).reshape(query_counts.shape[0], STATES * LANES)
    segment = lax.all_gather(query_rows, "db", axis=0, tiled=True)
    swap = [(q, q ^ 1) for q in range(query_count)]
    other = lax.ppermute(segment, "query", swap)

    idf_pad = pad_features(idf_weights)
    tables = []
    for step in range(chips):
        if step == 0:
            shard, shard_ids = logits, entry_ids
        else:
            ring = [(q, (q + CORES * step) % query_count) for q in range(query_count)]
            shard = lax.ppermute(logits, "query", ring)
            shard_ids = lax.ppermute(entry_ids, "query", ring)
        tables.append(encode(shard, shard_ids, idf_pad, rows, db_count))

    def best(table, queries):
        scores = lax.dot_general(
            table, queries, (((1,), (1,)), ((), ())), preferred_element_type=jnp.float32
        )
        return jnp.max(scores.reshape(rows // db_count, db_count, queries.shape[0]), axis=0)

    def halves(queries):
        parts = [best(table, queries) for table in tables]
        places = [(chip - step) % chips * HALVES // chips for step in range(chips)]
        return jnp.stack(
            [
                functools.reduce(
                    jnp.maximum,
                    [jnp.where(place == half, part, -jnp.inf) for place, part in zip(places, parts)],
                )
                for half in range(HALVES)
            ],
            axis=1,
        )

    mine = jnp.maximum(halves(segment), lax.ppermute(halves(other), "query", swap))
    arrived = lax.all_to_all(mine, "db", split_axis=0, concat_axis=0, tiled=True)
    return jnp.max(arrived, axis=0)


def solution(mesh):
    placed = (P(None, ("query", "db")), P(("query", "db")), P(("query", "db"), None), P())
    return jax.shard_map(
        on_device, mesh=mesh, in_specs=placed, out_specs=P("db", "query"), check_vma=False
    )
```

time: 288 us -> 194 us (0.67)
  other arithmetic: 84.6 us -> 3.92 us
  local copies, waits for them, and re-layouts: 47.4 us -> 5.5 us
  Pallas kernels: 0 us -> 38.6 us
  matrix products: 35.5 us -> 15.7 us
  waiting for transfers between devices: 86.1 us -> 99.4 us
  starting transfers between devices: 13.5 us -> 2.1 us
  blocking collectives: 0 us -> 9.5 us
  loops' own time: 5.37 us -> 0 us
  between operations: 14.2 us -> 18.8 us
    all_gather x1, waiting for transfers between devices: 0.02 us -> 89.7 us  [on_device(): segment = lax.all_gather(query_rows, 'db', axis=0, tiled=True)]
    scatter-add x8 -> x0, other arithmetic: 56 us -> none  [add_group(): counts_table = counts_table.at[targets].add(pair_sums.reshape(-1, FEAT))]
    all_to_all x2 -> x0, waiting for transfers between devices: 48 us -> none  [the longest x1 48 us: on_device(): lax.all_to_all(outgoing, 'db', split_axis=0, concat_axis=0, tiled=True)]
    pallas_call x0 -> x2, Pallas kernels: none -> 38.6 us  [encode(): pl.pallas_call(functools.partial(encode_kernel, residues, rows, chunk), o...]
    all_gather x1 -> x0, waiting for transfers between devices: 38.1 us -> none  [on_device(): replicas = lax.all_gather(owned_rows, 'query', axis=0, tiled=True)]
    reshape x25 -> x1, local copies, waits for them, and re-layouts: 26 us -> 0.68 us  [pad_features(): split = values.reshape(lead + (STATES, COLS))]
    dot_general x9 -> x4, matrix products: 35.5 us -> 15.7 us  [best(): lax.dot_general(table, queries, (((1,), (1,)), ((), ())), preferred_eleme...]
    all_to_all x2 -> x0, starting transfers between devices: 13.2 us -> none  [the longest x1 7.31 us: on_device(): lax.all_to_all(targets, 'db', split_axis=0, concat_axis=0, tiled=True)]
  transfers between devices with their start and end apart: 4 -> 5, of which waited for: 2 -> 3; matrix products, arithmetic and copies ran while one was open for 53% -> 4% of each run, Pallas kernels for 0% -> 20%
where the time goes in v1:
time: 194 us
  waiting for transfers between devices  99.4 us (51%)
  Pallas kernels  38.6 us (20%)
  between operations  18.8 us (10%)
  matrix products  15.7 us (8%)
  blocking collectives  9.5 us (5%)
  local copies, waits for them, and re-layouts  5.5 us (3%)
  other arithmetic  3.92 us (2%)
  starting transfers between devices  2.1 us (1%)
    all_gather x1, waiting for transfers between devices, on_device(): segment = lax.all_gather(query_rows, 'db', axis=0, tiled=True)  89.7 us
    pallas_call x2, Pallas kernels, encode(): pl.pallas_call(functools.partial(encode_kernel, residues, rows, chunk), o...  38.6 us
    dot_general x4, matrix products, best(): lax.dot_general(table, queries, (((1,), (1,)), ((), ())), preferred_eleme...  15.7 us
    all_to_all x1, blocking collectives, on_device(): lax.all_to_all(mine, 'db', split_axis=0, concat_axis=0, tiled=True)  9.5 us
    ppermute x1, waiting for transfers between devices, on_device(): shard = lax.ppermute(logits, 'query', ring)  8.46 us
  transfers between devices with their start and end apart: 5, of which 3 were waited for; matrix products, arithmetic and copies ran while one was open for 4% of the time, Pallas kernels for 20%

profile of v1, /device:TPU:0, one launch (start us, length us, event | category | flops | bytes accessed | tf_op | source)
XLA Modules:
  0.0 193.5 jit_solution(17289694587741475042)
XLA Ops:
  6.5 0.0 copy-start.4
  6.5 0.0 copy-start.3
  6.5 0.0 copy-start
  6.5 0.0 all-gather.2.cloned.1.call-start
  6.5 1.6 multiply_reduce_fusion
  8.2 1.5 divide_convert_fusion
  9.6 0.9 pad.17
  10.6 0.0 all-gather.2.cloned.1.call-update
  10.6 89.7 %all-gather.2.cloned.1.call-done = bf16[1024,2560]{0,1:T(8,128)(2,1)} async-done(((bf16[128,2560]{0,1:T(8,128)(2,1)}), bf16[1024,2560]{0,1:T(8,128)(2,1)}) %all-gather.2.cloned.1.call-update) | async-done | bytes 5242896 | tf_op jit(solution)/shard_map/all_gather | solution.py:144
  100.3 0.0 collective-permute-start.2
  100.3 0.0 copy-done.3
  100.3 1.5 collective-permute-start
  101.8 0.0 copy-done
  101.8 0.5 collective-permute-start.1
  102.3 0.5 slice.12
  104.1 0.0 copy-done.4
  104.1 0.7 reshape.124
  106.1 0.2 slice.13
  106.3 0.1 broadcast_in_dim.19.ids_ref
  106.4 0.7 pad.16.idf_ref
  107.2 19.3 %encode.2 = bf16[464,2560]{1,0:T(8,128)(2,1)S(1)} custom-call(s32[128]{0:T(128)S(1)} %multiply_clamp_fusion.1.starts_ref, bf16[20,32768]{1,0:T(8,128)(2,1)S(1)} %copy-done, s32[1,32896]{1,0:T(1,128)S(1)} %broadcast_in_dim.19.ids_ref, f32[20,128]{1,0:T(8,128)S(1)} %pad.16.idf_ref), custom_call_target="tpu_custom_call" | custom-call | flops 2684354560 | bytes 3817472 | tf_op jit(solution)/shard_map/encode/pallas_call | solution.py:104
  126.5 0.0 copy-start.1
  126.5 1.4 copy-done.1
  127.9 0.0 collective-permute-done
  127.9 0.5 slice.16
  131.0 0.2 slice.15
  131.3 0.1 broadcast_in_dim.21.ids_ref
  131.4 0.0 slice-start
  131.4 0.0 slice-start.1
  131.4 8.5 %collective-permute-done.1.logits_ref = bf16[20,32768]{1,0:T(8,128)(2,1)S(1)} collective-permute-done((bf16[20,32768]{1,0:T(8,128)(2,1)S(1)}, bf16[20,32768]{1,0:T(8,128)(2,1)S(1)}, u32[]{:S(2)}, u32[]{:S(2)}) %collective-permute-start.1) | collective-permute-done | bytes 1310752 | tf_op jit(solution)/shard_map/ppermute | solution.py:155
  139.9 19.3 %encode.3 = bf16[464,2560]{1,0:T(8,128)(2,1)S(1)} custom-call(s32[128]{0:T(128)S(1)} %multiply_clamp_fusion.starts_ref, bf16[20,32768]{1,0:T(8,128)(2,1)S(1)} %collective-permute-done.1.logits_ref, s32[1,32896]{1,0:T(1,128)S(1)} %broadcast_in_dim.21.ids_ref, f32[20,128]{1,0:T(8,128)S(1)} %pad.16.idf_ref), custom_call_target="tpu_custom_call" | custom-call | flops 2684354560 | bytes 3817472 | tf_op jit(solution)/shard_map/encode/pallas_call | solution.py:104
  159.2 0.0 slice-done
  159.2 0.0 slice-done.1
  159.2 0.0 copy-start.2
  159.2 2.7 %bitcast_reduce_fusion.2 = f32[8,1024]{1,0:T(8,128)S(1)} fusion(bf16[464,2560]{1,0:T(8,128)(2,1)S(1)} %encode.3, bf16[1024,2560]{0,1:T(8,128)(2,1)S(1)} %bitcast.29), kind=kOutput, calls=%fused_computation.2 | convolution fusion | flops 2433163264 | bytes 7651328 | tf_op jit(solution)/shard_map/dot_general | solution.py:160
  162.0 0.0 copy-done.2
  162.0 2.6 %bitcast_reduce_fusion.3 = f32[8,1024]{1,0:T(8,128)S(1)} fusion(bf16[464,2560]{1,0:T(8,128)(2,1)S(1)} %copy-done.2, bf16[1024,2560]{0,1:T(8,128)(2,1)S(1)} %bitcast.29), kind=kOutput, calls=%fused_computation.3 | convolution fusion | flops 2433163264 | bytes 7651328 | tf_op jit(solution)/shard_map/dot_general | solution.py:160
  164.6 0.0 collective-permute-done.2
  164.6 5.2 %bitcast_reduce_fusion = f32[8,1024]{1,0:T(8,128)S(1)} fusion(bf16[464,2560]{1,0:T(8,128)(2,1)S(1)} %encode.3, bf16[1024,2560]{0,1:T(8,128)(2,1)} %collective-permute-done.2), kind=kOutput, calls=%fused_computation | convolution fusion | flops 2433163264 | bytes 7651328 | tf_op jit(solution)/shard_map/dot_general | solution.py:160
  169.9 5.1 %bitcast_reduce_fusion.1 = f32[8,1024]{1,0:T(8,128)S(1)} fusion(bf16[464,2560]{1,0:T(8,128)(2,1)S(1)} %copy-done.2, bf16[1024,2560]{0,1:T(8,128)(2,1)} %collective-permute-done.2), kind=kOutput, calls=%fused_computation.1 | convolution fusion | flops 2433163264 | bytes 7651328 | tf_op jit(solution)/shard_map/dot_general | solution.py:160
  175.1 0.1 pad_maximum_fusion.1
  175.1 0.1 collective-permute-start.3
  175.2 1.2 collective-permute-done.3
  176.5 0.1 copy_maximum_fusion
  176.5 9.5 %all_to_all.5 = f32[8,2,1024]{2,1,0:T(2,128)S(1)} all-to-all(f32[8,2,1024]{2,1,0:T(2,128)S(1)} %copy_maximum_fusion), channel_id=1, replica_groups=mesh['query'=4,'db'=8] {'db'}, dimensions={0} | all-to-all | bytes 131072 | tf_op jit(solution)/shard_map/all_to_all | solution.py:180
  186.0 0.6 reduce_max.49
  (13 shorter events, 0.2 us)
Async XLA Ops:
  6.5 97.6 %copy-start.4 = (f32[2400]{0:T(1024)S(1)}, f32[2400]{0:T(1024)}, u32[]{:S(2)}) copy-start(f32[2400]{0:T(1024)} %param.7) | copy-start | bytes 28804
  6.5 93.7 %copy-start.3 = (s32[32768]{0:T(1024)S(1)}, s32[32768]{0:T(1024)}, u32[]{:S(2)}) copy-start(s32[32768]{0:T(1024)} %param.5) | copy-start | bytes 393220
  6.5 95.2 %copy-start = (bf16[20,32768]{1,0:T(8,128)(2,1)S(1)}, bf16[20,32768]{1,0:T(8,128)(2,1)}, u32[]{:S(2)}) copy-start(bf16[20,32768]{1,0:T(8,128)(2,1)} %logits_ref.1) | copy-start | bytes 3932164
  6.5 93.7 %all-gather.2.cloned.1.call-start = ((), (), s32[]{:S(2)}) async-start(), calls=%async_computation.1 | async-start | bytes 5898240 | tf_op jit(solution)/shard_map/all_gather | solution.py:144
  100.3 64.4 %collective-permute-start.2 = (bf16[1024,2560]{0,1:T(8,128)(2,1)}, bf16[1024,2560]{0,1:T(8,128)(2,1)}, u32[]{:S(2)}, u32[]{:S(2)}) collective-permute-start(bf16[1024,2560]{0,1:T(8,128)(2,1)} %all-gather.2.cloned.1.call-done), channel_id=1, source_target_pairs={{0,8},{8,0},{16,24},{24,16},{1,9},{9,1},{17,25},{25,17},{2,10},{10... | collective-permute-start | bytes 15728648 | tf_op jit(solution)/shard_map/ppermute | solution.py:146
  100.3 27.7 %collective-permute-start = (s32[32768]{0:T(1024)S(1)}, s32[32768]{0:T(1024)S(1)}, u32[]{:S(2)}, u32[]{:S(2)}) collective-permute-start(s32[32768]{0:T(1024)S(1)} %copy-done.3), channel_id=1, source_target_pairs={{0,16},{8,24},{16,0},{24,8},{1,17},{9,25},{17,1},{25,9},{2,18},{10... | collective-permute-start | bytes 393224 | tf_op jit(solution)/shard_map/ppermute | solution.py:156
  101.8 38.1 %collective-permute-start.1 = (bf16[20,32768]{1,0:T(8,128)(2,1)S(1)}, bf16[20,32768]{1,0:T(8,128)(2,1)S(1)}, u32[]{:S(2)}, u32[]{:S(2)}) collective-permute-start(bf16[20,32768]{1,0:T(8,128)(2,1)S(1)} %copy-done), channel_id=1, source_target_pairs={{0,16},{8,24},{16,0},{24,8},{1,17},{9,25},{17,1},{25,9},{2,18},{10... | collective-permute-start | bytes 3932168 | tf_op jit(solution)/shard_map/ppermute | solution.py:155
  126.5 1.4 copy-start.1
  131.4 27.8 %slice-start = ((s8[5242880]{0:T(1024)(128)(4,1)}), s8[4194304]{0:T(1024)(128)(4,1)S(1)}, s32[]{:S(2)}) async-start(s8[5242880]{0:T(1024)(128)(4,1)} %bitcast.28), calls=%async_computation.2 | async-start | bytes 8388608
  131.4 27.8 %slice-start.1 = ((s8[5242880]{0:T(1024)(128)(4,1)}), s8[1048576]{0:T(1024)(128)(4,1)S(1)}, s32[]{:S(2)}) async-start(s8[5242880]{0:T(1024)(128)(4,1)} %bitcast.28), calls=%async_computation.3 | async-start | bytes 2097152
  159.2 2.8 %copy-start.2 = (bf16[464,2560]{1,0:T(8,128)(2,1)S(1)}, bf16[464,2560]{1,0:T(8,128)(2,1)}, u32[]{:S(2)}) copy-start(bf16[464,2560]{1,0:T(8,128)(2,1)} %copy-done.1) | copy-start | bytes 7127044
  175.1 1.3 collective-permute-start.3
Sparse Core Ops, SparseCore 0:
  10.7 89.4 all-gather.1
